TPU v7x, 256 devices: a whole 4x4x8 slice. The times are simulated.
256 devices in a mesh: gx: 8 (over y, x_lo), gy: 4 (over x_hi, core), gz: 8 (over z).
Axes of the slice: x: 4 (x_hi: 2, x_lo: 2; x = x_hi * 2 + x_lo), y: 4, z: 8, core: 2. Of those that a mesh axis runs over, the one named last changes fastest.
Arguments:
- tensor_blocks: bfloat16 [8, 4, 8, 3, 128, 128, 128], P('gx', 'gy', 'gz'), may hold values from 0 to 3
- fiber_mask: int32 [8, 4, 8, 3, 128, 128], P('gx', 'gy', 'gz'), may hold values 0 or 1
- block_coords: int32 [8, 4, 8, 3, 3], P('gx', 'gy', 'gz'), may hold values from 0 to 7, as said below
- block_counts: int32 [8, 4, 8], P('gx', 'gy', 'gz'), may hold values from 0 to 3, as said below
- factor_a: bfloat16 [8, 512, 256], P('gx', ('gy', 'gz')), may hold values from -0.59765625 to 0.59765625
- factor_b: bfloat16 [4, 1024, 256], P('gy', ('gx', 'gz')), may hold values from -0.59765625 to 0.59765625
- factor_c: bfloat16 [8, 512, 256], P('gz', ('gx', 'gy')), may hold values from -0.59765625 to 0.59765625
Outputs:
- grad_a: float32 [8, 512, 256], P('gx', ('gy', 'gz'))
- grad_b: float32 [4, 1024, 256], P('gy', ('gx', 'gz'))
- grad_c: float32 [8, 512, 256], P('gz', ('gx', 'gy'))
Inputs may be any that keep to these rules, and one draw needn't show every extreme that they name: `block_counts`: some sub-box holds exactly 3 blocks and some holds none, in every draw; slots at and past a sub-box's count hold no block. `block_coords`: the 3 columns of one sub-box name distinct blocks; row 0 is below 4, row 1 below 8, row 2 below 4.
All inputs are finite; a program needn't handle non-finite values. No bound on the sum of `fiber_mask` on one device may be relied on, other than what follows from the above.
Results may differ from a plain program's by a relative error of at most 0.0014.
Values may be sent and summed in bfloat16 or wider, within the bound.
A program may use at most 128 MiB of HBM per device.

v0:
```python
from functools import partial
import jax
import jax.numpy as jnp
from jax import lax
from jax.sharding import PartitionSpec as P

R = 256
BLK = 128
SLOTS = 3


def block_terms(rows_a, rows_b, rows_c, entries, fibers):
    khatri = (
        rows_b[:, None, :].astype(jnp.float32) * rows_c[None, :, :].astype(jnp.float32)
    ).astype(jnp.bfloat16)
    khatri = khatri.reshape(BLK * BLK, R)
    log_rate = jnp.einsum("ur,kr->uk", rows_a, khatri, preferred_element_type=jnp.float32)
    weight = fibers.astype(jnp.float32).reshape(BLK, BLK, 1)
    misfit = weight * (jnp.exp(log_rate.reshape(BLK, BLK, BLK)) - entries.astype(jnp.float32)) / BLK
    misfit = misfit.astype(jnp.bfloat16).reshape(BLK, BLK * BLK)
    part_a = jnp.dot(misfit, khatri, preferred_element_type=jnp.float32)
    folded = jnp.einsum("uk,ur->kr", misfit, rows_a, preferred_element_type=jnp.float32)
    folded = folded.astype(jnp.bfloat16).reshape(BLK, BLK, R)
    part_b = jnp.einsum("vwr,wr->vr", folded, rows_c, preferred_element_type=jnp.float32)
    part_c = jnp.einsum("vwr,vr->wr", folded, rows_b, preferred_element_type=jnp.float32)
    return (part_a, part_b, part_c)


def add_rows(total, start, part):
    current = lax.dynamic_slice_in_dim(total, start, BLK, 0)
    return lax.dynamic_update_slice_in_dim(total, current + part, start, 0)


def add_block(slot_index, coords, tensor_blocks, fiber_mask, slabs, totals):
    slab_rows_a, slab_rows_b, slab_rows_c = slabs
    grad_a, grad_b, grad_c = totals
    start_a = coords[0, slot_index] * BLK
    start_b = coords[1, slot_index] * BLK
    start_c = coords[2, slot_index] * BLK
    rows_a = lax.dynamic_slice_in_dim(slab_rows_a, start_a, BLK, 0)
    rows_b = lax.dynamic_slice_in_dim(slab_rows_b, start_b, BLK, 0)
    rows_c = lax.dynamic_slice_in_dim(slab_rows_c, start_c, BLK, 0)
    entries = tensor_blocks[0, 0, 0, slot_index]
    fibers = fiber_mask[0, 0, 0, slot_index]
    part_a, part_b, part_c = block_terms(rows_a, rows_b, rows_c, entries, fibers)
    return (
        add_rows(grad_a, start_a, part_a),
        add_rows(grad_b, start_b, part_b),
        add_rows(grad_c, start_c, part_c),
    )


def keep_totals(totals):
    return totals


def per_device(tensor_blocks, fiber_mask, block_coords, block_counts, factor_a, factor_b, factor_c):
    slab_rows_a = lax.all_gather(factor_a, ("gy", "gz"), axis=1, tiled=True)[0]
    slab_rows_b = lax.all_gather(factor_b, ("gx", "gz"), axis=1, tiled=True)[0]
    slab_rows_c = lax.all_gather(factor_c, ("gx", "gy"), axis=1, tiled=True)[0]
    slabs = (slab_rows_a, slab_rows_b, slab_rows_c)
    filled = block_counts[0, 0, 0]
    coords = block_coords[0, 0, 0]
    totals = (
        jnp.zeros(slab_rows_a.shape, jnp.float32),
        jnp.zeros(slab_rows_b.shape, jnp.float32),
        jnp.zeros(slab_rows_c.shape, jnp.float32),
    )
    for slot_index in range(SLOTS):
        adder = partial(add_block, slot_index, coords, tensor_blocks, fiber_mask, slabs)
        totals = lax.cond(slot_index < filled, adder, keep_totals, totals)
    terms_a, terms_b, terms_c = totals
    grad_a = lax.psum_scatter(terms_a[None], ("gy", "gz"), scatter_dimension=1, tiled=True)
    grad_b = lax.psum_scatter(terms_b[None], ("gx", "gz"), scatter_dimension=1, tiled=True)
    grad_c = lax.psum_scatter(terms_c[None], ("gx", "gy"), scatter_dimension=1, tiled=True)
    return (grad_a, grad_b, grad_c)


def solution(mesh):
    placed = (
        P("gx", "gy", "gz", None, None, None, None),
        P("gx", "gy", "gz", None, None, None),
        P("gx", "gy", "gz", None, None),
        P("gx", "gy", "gz"),
        P("gx", ("gy", "gz"), None),
        P("gy", ("gx", "gz"), None),
        P("gz", ("gx", "gy"), None),
    )
    return jax.shard_map(
        per_device,
        mesh=mesh,
        in_specs=placed,
        out_specs=(
            P("gx", ("gy", "gz"), None),
            P("gy", ("gx", "gz"), None),
            P("gz", ("gx", "gy"), None),
        ),
        check_vma=False,
    )
```

profile of v0, /device:TPU:4, one launch (start us, length us, event | category | flops | bytes accessed | tf_op | source)
XLA Modules:
  0.0 951.6 jit_solution(9491583259348897552)
XLA Ops:
  7.2 0.0 reduce-scatter.4.cloned.1.call-start
  7.2 161.8 %all_gather.10 = bf16[1,1024,256]{2,1,0:T(8,128)(2,1)S(1)} all-gather(bf16[1,16,256]{2,1,0:T(8,128)(2,1)} %param.18), channel_id=1, replica_groups=mesh['gx'=8,'gy'=4,'gz'=8] {'gx','gz'}, dimensions={1}, use_global_device_ids=true | all-gather | bytes 532480 | tf_op jit(solution)/shard_map/all_gather | solution.py:59
  169.0 65.1 %all_gather.9 = bf16[1,512,256]{2,1,0:T(8,128)(2,1)S(1)} all-gather(bf16[1,16,256]{2,1,0:T(8,128)(2,1)} %param.17), channel_id=1, replica_groups=mesh['gx'=8,'gy'=4,'gz'=8] {'gy','gz'}, dimensions={1}, use_global_device_ids=true | all-gather | bytes 270336 | tf_op jit(solution)/shard_map/all_gather | solution.py:58
  234.1 36.9 %all_gather.11 = bf16[1,512,256]{2,1,0:T(8,128)(2,1)S(1)} all-gather(bf16[1,16,256]{2,1,0:T(8,128)(2,1)} %param.19), channel_id=1, replica_groups=mesh['gx'=8,'gy'=4,'gz'=8] {'gx','gy'}, dimensions={1}, use_global_device_ids=true | all-gather | bytes 270336 | tf_op jit(solution)/shard_map/all_gather | solution.py:60
  271.0 0.7 copy.72
  272.4 36.4 %conditional.3 = (f32[512,256]{1,0:T(8,128)}, f32[1024,256]{1,0:T(8,128)}, f32[512,256]{1,0:T(8,128)}) conditional(s32[]{:T(128)} %bitcast.53, () %tuple.28, (s32[1,1,1,3,128,128]{5,4,3,2,1,0:T(8,128)}, s32[3,3]{1,0:T(4,128)S(1)}, bf16[512,256]{1,0:T(8,128)(2,1)S(1)}, bf16[1024,256]{1,0:T(8,128)(2,1)S(1)}, bf16[512,256]{1,0:T(8,128)(2,1)S(1)}, ...), branch_computations={%region_0.0_spmd, %region_1.0_spmd} | conditional | flops 3277930496 | bytes 64684284 | solution.py:71
  272.4 0.6 fusion.57
  274.9 0.0 copy-start
  274.9 17.6 %copy.14 = bf16[1,1,1,3,128,128,128]{4,6,5,3,2,1,0:T(8,128)(2,1)} copy(bf16[1,1,1,3,128,128,128]{6,5,4,3,2,1,0:T(8,128)(2,1)} %get-tuple-element.110) | data formatting | bytes 25165824 | tf_op jit(solution)/shard_map
  292.5 0.0 copy-done
  292.5 0.1 copy.13
  292.6 4.7 fusion.4
  297.3 2.6 multiply_reduce_fusion.1
  299.9 1.1 broadcast_in_dim.12
  301.0 0.7 bitcast_dynamic-update-slice_fusion.1
  301.7 2.8 multiply_reduce_fusion
  304.4 0.8 broadcast.26.clone.1
  305.3 0.7 bitcast_dynamic-update-slice_fusion
  305.9 0.8 broadcast.26.clone
  306.7 2.0 fusion.10
  308.8 34.9 %conditional.4 = ((f32[512,256]{1,0:T(8,128)}, f32[1024,256]{1,0:T(8,128)}, f32[512,256]{1,0:T(8,128)})) conditional(s32[]{:T(128)} %bitcast.52, (f32[512,256]{1,0:T(8,128)}, f32[1024,256]{1,0:T(8,128)}, f32[512,256]{1,0:T(8,128)}) %conditional.3, (s32[3,3]{1,0:T(4,128)S(1)}, f32[512,256]{1,0:T(8,128)}, s32[1,1,1,3,128,128]{5,4,3,2,1,0:T(8,128)}, ...), branch_computations={%region_2.0_spmd, %region_3.0_spmd} | conditional | flops 3278028800 | bytes 62980344 | solution.py:71
  308.8 0.6 fusion.58
  311.3 0.0 copy-start.1
  311.3 17.6 %copy.16 = bf16[1,1,1,3,128,128,128]{4,6,5,3,2,1,0:T(8,128)(2,1)} copy(bf16[1,1,1,3,128,128,128]{6,5,4,3,2,1,0:T(8,128)(2,1)} %get-tuple-element.117) | data formatting | bytes 25165824 | tf_op jit(solution)/shard_map
  328.8 0.0 copy-done.1
  328.8 0.1 copy.15
  329.0 4.7 fusion.21
  333.7 2.6 multiply_reduce_fusion.3
  336.3 2.8 multiply_reduce_fusion.2
  339.0 1.7 fusion.29
  340.7 2.9 fusion.28
  343.7 0.0 reduce-scatter.4.cloned.1.call-update
  343.7 0.0 reduce-scatter.8.cloned.1.call-start
  343.8 0.7 reduce-scatter.8.cloned.1.call-update
  344.5 0.0 reduce-scatter.6.cloned.1.call-start
  344.5 0.7 reduce-scatter.6.cloned.1.call-update
  345.2 142.6 %reduce-scatter.4.cloned.1.call-done = f32[1,16,256]{2,1,0:T(8,128)} async-done(((f32[1,512,256]{2,1,0:T(8,128)}), f32[1,16,256]{2,1,0:T(8,128)}) %reduce-scatter.4.cloned.1.call-update) | async-done | bytes 16400 | tf_op jit(solution)/shard_map/reduce_scatter | solution.py:73
  487.8 133.6 %reduce-scatter.8.cloned.1.call-done = f32[1,16,256]{2,1,0:T(8,128)} async-done(((f32[1,512,256]{2,1,0:T(8,128)}), f32[1,16,256]{2,1,0:T(8,128)}) %reduce-scatter.8.cloned.1.call-update) | async-done | bytes 16400 | tf_op jit(solution)/shard_map/reduce_scatter | solution.py:75
  621.4 323.7 %reduce-scatter.6.cloned.1.call-done = f32[1,16,256]{2,1,0:T(8,128)} async-done(((f32[1,1024,256]{2,1,0:T(8,128)}), f32[1,16,256]{2,1,0:T(8,128)}) %reduce-scatter.6.cloned.1.call-update) | async-done | bytes 16400 | tf_op jit(solution)/shard_map/reduce_scatter | solution.py:74
  (6 shorter events, 0.1 us)
Async XLA Ops:
  7.2 480.7 %reduce-scatter.4.cloned.1.call-start = ((), (), s32[]{:S(2)}) async-start(), calls=%async_computation.3 | async-start | bytes 540672 | tf_op jit(solution)/shard_map/reduce_scatter | solution.py:73
  274.9 17.6 %copy-start = (s32[1,1,1,3,128,128]{5,4,3,2,1,0:T(8,128)S(1)}, s32[1,1,1,3,128,128]{5,4,3,2,1,0:T(8,128)}, u32[]{:S(2)}) copy-start(s32[1,1,1,3,128,128]{5,4,3,2,1,0:T(8,128)} %get-tuple-element.105) | copy-start | bytes 589828 | tf_op jit(solution)/shard_map/cond
  311.3 17.6 %copy-start.1 = (s32[1,1,1,3,128,128]{5,4,3,2,1,0:T(8,128)S(1)}, s32[1,1,1,3,128,128]{5,4,3,2,1,0:T(8,128)}, u32[]{:S(2)}) copy-start(s32[1,1,1,3,128,128]{5,4,3,2,1,0:T(8,128)} %get-tuple-element.113) | copy-start | bytes 589828 | tf_op jit(solution)/shard_map/cond
  343.7 277.7 %reduce-scatter.8.cloned.1.call-start = ((), (), s32[]{:S(2)}) async-start(), calls=%async_computation.5 | async-start | bytes 540672 | tf_op jit(solution)/shard_map/reduce_scatter | solution.py:75
  344.5 600.7 %reduce-scatter.6.cloned.1.call-start = ((), (), s32[]{:S(2)}) async-start(), calls=%async_computation.4 | async-start | bytes 1064960 | tf_op jit(solution)/shard_map/reduce_scatter | solution.py:74
Sparse Core Ops, SparseCore 0:
  343.8 143.9 reduce-scatter.3
  490.9 130.5 reduce-scatter.7
  624.5 320.5 reduce-scatter.5
where the time goes:
time: 953 us; the launch traced here: 952 us
  waiting for transfers between devices  601 us (63%)
  blocking collectives  264 us (28%)
  local copies, waits for them, and re-layouts  41.3 us (4%)
  matrix products  19.5 us (2%)
  between operations  14.4 us (2%)
    reduce_scatter x1, waiting for transfers between devices, per_device(): lax.psum_scatter(terms_b[None], ('gx', 'gz'), scatter_dimension=1, tiled=...  324 us
    all_gather x1, blocking collectives, per_device(): slab_rows_b = lax.all_gather(factor_b, ('gx', 'gz'), axis=1, tiled=True)[0]  162 us
    reduce_scatter x1, waiting for transfers between devices, per_device(): lax.psum_scatter(terms_a[None], ('gy', 'gz'), scatter_dimension=1, tiled=...  143 us
    reduce_scatter x1, waiting for transfers between devices, per_device(): lax.psum_scatter(terms_c[None], ('gx', 'gy'), scatter_dimension=1, tiled=...  134 us
    all_gather x1, blocking collectives, per_device(): slab_rows_a = lax.all_gather(factor_a, ('gy', 'gz'), axis=1, tiled=True)[0]  65.1 us
    another operation x6, local copies, waits for them, and re-layouts  37 us
    all_gather x1, blocking collectives, per_device(): slab_rows_c = lax.all_gather(factor_c, ('gx', 'gy'), axis=1, tiled=True)[0]  36.9 us
  transfers between devices with their start and end apart: 3, of which 3 were waited for; matrix products, arithmetic and copies ran while one was open for 0% of the time, Pallas kernels for 0%

commit v1 on v0

--- a/solution.py
+++ b/solution.py
@@ -56,7 +56,10 @@
 
 def per_device(tensor_blocks, fiber_mask, block_coords, block_counts, factor_a, factor_b, factor_c):
     slab_rows_a = lax.all_gather(factor_a, ("gy", "gz"), axis=1, tiled=True)[0]
-    slab_rows_b = lax.all_gather(factor_b, ("gx", "gz"), axis=1, tiled=True)[0]
+    slab_rows_b = jnp.concatenate(
+        lax.all_to_all(jnp.stack([factor_b] * lax.axis_size(("gx", "gz"))), ("gx", "gz"), 0, 0),
+        axis=1,
+    )[0]
     slab_rows_c = lax.all_gather(factor_c, ("gx", "gy"), axis=1, tiled=True)[0]
     slabs = (slab_rows_a, slab_rows_b, slab_rows_c)
     filled = block_counts[0, 0, 0]

time: 953 us -> 813 us (0.85)
  blocking collectives: 264 us -> 110 us
  starting transfers between devices: 0.12 us -> 12.9 us
    all_gather x1 -> x0, blocking collectives: 162 us -> none  [per_device(): slab_rows_b = lax.all_gather(factor_b, ('gx', 'gz'), axis=1, tiled=True)[0]]
    all_to_all x0 -> x1, starting transfers between devices: none -> 12.7 us  [per_device(): lax.all_to_all(jnp.stack([factor_b] * lax.axis_size(('gx', 'gz'))), ('gx'...]
    another operation x6 -> x7, local copies, waits for them, and re-layouts: 37 us -> 38.5 us
  transfers between devices with their start and end apart: 3 -> 4, of which waited for: 3 -> 3; matrix products, arithmetic and copies ran while one was open for 0% -> 0% of each run, Pallas kernels for 0% -> 0%
where the time goes in v1:
time: 813 us; the launch traced here: 812 us
  waiting for transfers between devices  601 us (74%)
  blocking collectives  110 us (14%)
  local copies, waits for them, and re-layouts  42.8 us (5%)
  matrix products  19.5 us (2%)
  between operations  14.4 us (2%)
  starting transfers between devices  12.9 us (2%)
    reduce_scatter x1, waiting for transfers between devices, per_device(): lax.psum_scatter(terms_b[None], ('gx', 'gz'), scatter_dimension=1, tiled=...  325 us
    reduce_scatter x1, waiting for transfers between devices, per_device(): lax.psum_scatter(terms_a[None], ('gy', 'gz'), scatter_dimension=1, tiled=...  141 us
    reduce_scatter x1, waiting for transfers between devices, per_device(): lax.psum_scatter(terms_c[None], ('gx', 'gy'), scatter_dimension=1, tiled=...  134 us
    all_gather x1, blocking collectives, per_device(): slab_rows_a = lax.all_gather(factor_a, ('gy', 'gz'), axis=1, tiled=True)[0]  71.7 us
    all_gather x1, blocking collectives, per_device(): slab_rows_c = lax.all_gather(factor_c, ('gx', 'gy'), axis=1, tiled=True)[0]  38.1 us
    another operation x6, local copies, waits for them, and re-layouts  36.9 us
  transfers between devices with their start and end apart: 4, of which 3 were waited for; matrix products, arithmetic and copies ran while one was open for 0% of the time, Pallas kernels for 0%

profile of v1, /device:TPU:4, one launch (start us, length us, event | category | flops | bytes accessed | tf_op | source)
XLA Modules:
  0.0 811.8 jit_solution(13700120536310571257)
XLA Ops:
  7.2 1.5 stack.2
  8.7 12.7 %all-to-all-start = ((bf16[64,1,16,256]{3,2,1,0:T(8,128)(2,1)}), bf16[64,1,16,256]{3,2,1,0:T(8,128)(2,1)S(1)}, u32[]{:S(2)}, u32[]{:S(2)}) async-start(bf16[64,1,16,256]{3,2,1,0:T(8,128)(2,1)} %stack.2), calls=%async_computation | async-start | bytes 1048576 | tf_op jit(solution)/shard_map/all_to_all | solution.py:60
  21.4 0.0 reduce-scatter.4.cloned.1.call-start
  21.5 0.7 copy.81
  22.8 71.7 %all_gather.6 = bf16[1,512,256]{2,1,0:T(8,128)(2,1)S(1)} all-gather(bf16[1,16,256]{2,1,0:T(8,128)(2,1)} %param.17), channel_id=1, replica_groups=mesh['gx'=8,'gy'=4,'gz'=8] {'gy','gz'}, dimensions={1}, use_global_device_ids=true | all-gather | bytes 270336 | tf_op jit(solution)/shard_map/all_gather | solution.py:58
  94.6 38.1 %all_gather.7 = bf16[1,512,256]{2,1,0:T(8,128)(2,1)S(1)} all-gather(bf16[1,16,256]{2,1,0:T(8,128)(2,1)} %param.19), channel_id=1, replica_groups=mesh['gx'=8,'gy'=4,'gz'=8] {'gx','gy'}, dimensions={1}, use_global_device_ids=true | all-gather | bytes 270336 | tf_op jit(solution)/shard_map/all_gather | solution.py:63
  132.7 0.0 all-to-all-done
  132.7 36.4 %conditional.3 = (f32[512,256]{1,0:T(8,128)}, f32[1024,256]{1,0:T(8,128)}, f32[512,256]{1,0:T(8,128)}) conditional(s32[]{:T(128)} %bitcast.53, () %tuple.28, (s32[1,1,1,3,128,128]{5,4,3,2,1,0:T(8,128)}, s32[3,3]{1,0:T(4,128)S(1)}, bf16[512,256]{1,0:T(8,128)(2,1)S(1)}, bf16[1024,256]{1,0:T(8,128)(2,1)S(1)}, bf16[512,256]{1,0:T(8,128)(2,1)S(1)}, ...), branch_computations={%region_0.0_spmd, %region_1.0_spmd} | conditional | flops 3277930496 | bytes 64684284 | solution.py:74
  132.7 0.6 fusion.57
  135.3 0.0 copy-start
  135.3 17.5 %copy.23 = bf16[1,1,1,3,128,128,128]{4,6,5,3,2,1,0:T(8,128)(2,1)} copy(bf16[1,1,1,3,128,128,128]{6,5,4,3,2,1,0:T(8,128)(2,1)} %get-tuple-element.134) | data formatting | bytes 25165824 | tf_op jit(solution)/shard_map
  152.8 0.0 copy-done
  152.8 0.1 copy.22
  153.0 4.7 fusion.4
  157.7 2.6 multiply_reduce_fusion.1
  160.3 1.1 broadcast_in_dim.12
  161.4 0.7 bitcast_dynamic-update-slice_fusion.1
  162.0 2.8 multiply_reduce_fusion
  164.8 0.8 broadcast.29.clone.1
  165.6 0.7 bitcast_dynamic-update-slice_fusion
  166.3 0.8 broadcast.29.clone
  167.1 2.0 fusion.10
  169.1 35.0 %conditional.4 = ((f32[512,256]{1,0:T(8,128)}, f32[1024,256]{1,0:T(8,128)}, f32[512,256]{1,0:T(8,128)})) conditional(s32[]{:T(128)} %bitcast.52, (f32[512,256]{1,0:T(8,128)}, f32[1024,256]{1,0:T(8,128)}, f32[512,256]{1,0:T(8,128)}) %conditional.3, (s32[3,3]{1,0:T(4,128)S(1)}, f32[512,256]{1,0:T(8,128)}, s32[1,1,1,3,128,128]{5,4,3,2,1,0:T(8,128)}, ...), branch_computations={%region_2.0_spmd, %region_3.0_spmd} | conditional | flops 3278028800 | bytes 62980344 | solution.py:74
  169.1 0.7 fusion.58
  171.8 0.0 copy-start.1
  171.8 17.5 %copy.25 = bf16[1,1,1,3,128,128,128]{4,6,5,3,2,1,0:T(8,128)(2,1)} copy(bf16[1,1,1,3,128,128,128]{6,5,4,3,2,1,0:T(8,128)(2,1)} %get-tuple-element.141) | data formatting | bytes 25165824 | tf_op jit(solution)/shard_map
  189.3 0.0 copy-done.1
  189.3 0.1 copy.24
  189.5 4.7 fusion.21
  194.1 2.6 multiply_reduce_fusion.3
  196.8 2.8 multiply_reduce_fusion.2
  199.5 1.7 fusion.29
  201.2 2.9 fusion.28
  204.2 0.0 reduce-scatter.4.cloned.1.call-update
  204.2 0.0 reduce-scatter.8.cloned.1.call-start
  204.3 0.7 reduce-scatter.8.cloned.1.call-update
  205.0 0.0 reduce-scatter.6.cloned.1.call-start
  205.0 0.7 reduce-scatter.6.cloned.1.call-update
  205.7 141.2 %reduce-scatter.4.cloned.1.call-done = f32[1,16,256]{2,1,0:T(8,128)} async-done(((f32[1,512,256]{2,1,0:T(8,128)}), f32[1,16,256]{2,1,0:T(8,128)}) %reduce-scatter.4.cloned.1.call-update) | async-done | bytes 16400 | tf_op jit(solution)/shard_map/reduce_scatter | solution.py:76
  346.9 133.6 %reduce-scatter.8.cloned.1.call-done = f32[1,16,256]{2,1,0:T(8,128)} async-done(((f32[1,512,256]{2,1,0:T(8,128)}), f32[1,16,256]{2,1,0:T(8,128)}) %reduce-scatter.8.cloned.1.call-update) | async-done | bytes 16400 | tf_op jit(solution)/shard_map/reduce_scatter | solution.py:78
  480.6 324.7 %reduce-scatter.6.cloned.1.call-done = f32[1,16,256]{2,1,0:T(8,128)} async-done(((f32[1,1024,256]{2,1,0:T(8,128)}), f32[1,16,256]{2,1,0:T(8,128)}) %reduce-scatter.6.cloned.1.call-update) | async-done | bytes 16400 | tf_op jit(solution)/shard_map/reduce_scatter | solution.py:77
  (6 shorter events, 0.1 us)
Async XLA Ops:
  8.7 124.0 %all-to-all-start = ((bf16[64,1,16,256]{3,2,1,0:T(8,128)(2,1)}), bf16[64,1,16,256]{3,2,1,0:T(8,128)(2,1)S(1)}, u32[]{:S(2)}, u32[]{:S(2)}) async-start(bf16[64,1,16,256]{3,2,1,0:T(8,128)(2,1)} %stack.2), calls=%async_computation | async-start | bytes 1048576 | tf_op jit(solution)/shard_map/all_to_all | solution.py:60
  21.4 325.5 %reduce-scatter.4.cloned.1.call-start = ((), (), s32[]{:S(2)}) async-start(), calls=%async_computation.4 | async-start | bytes 540672 | tf_op jit(solution)/shard_map/reduce_scatter | solution.py:76
  135.3 17.5 %copy-start = (s32[1,1,1,3,128,128]{5,4,3,2,1,0:T(8,128)S(1)}, s32[1,1,1,3,128,128]{5,4,3,2,1,0:T(8,128)}, u32[]{:S(2)}) copy-start(s32[1,1,1,3,128,128]{5,4,3,2,1,0:T(8,128)} %get-tuple-element.129) | copy-start | bytes 589828 | tf_op jit(solution)/shard_map/cond
  171.8 17.5 %copy-start.1 = (s32[1,1,1,3,128,128]{5,4,3,2,1,0:T(8,128)S(1)}, s32[1,1,1,3,128,128]{5,4,3,2,1,0:T(8,128)}, u32[]{:S(2)}) copy-start(s32[1,1,1,3,128,128]{5,4,3,2,1,0:T(8,128)} %get-tuple-element.137) | copy-start | bytes 589828 | tf_op jit(solution)/shard_map/cond
  204.2 276.4 %reduce-scatter.8.cloned.1.call-start = ((), (), s32[]{:S(2)}) async-start(), calls=%async_computation.6 | async-start | bytes 540672 | tf_op jit(solution)/shard_map/reduce_scatter | solution.py:78
  205.0 600.3 %reduce-scatter.6.cloned.1.call-start = ((), (), s32[]{:S(2)}) async-start(), calls=%async_computation.5 | async-start | bytes 1064960 | tf_op jit(solution)/shard_map/reduce_scatter | solution.py:77
Sparse Core Ops, SparseCore 0:
  204.3 142.5 reduce-scatter.3
  350.0 130.5 reduce-scatter.7
  483.6 321.6 reduce-scatter.5
